TPU v7x, 128 devices: a whole 4x4x4 slice. The times are simulated.
128 devices in a mesh: layer: 4 (over z), row: 32 (over y, x, core).
Axes of the slice: x: 4, y: 4, z: 4, core: 2. Of those that a mesh axis runs over, the one named last changes fastest.
Arguments:
- rhs_sub: float32 [4, 3, 4096, 256], P('layer', None, 'row'), may hold values from -6 to 6
- rhs_root: float32 [2048, 256], P('row'), may hold values from -6 to 6
- lower_inv: float32 [4, 3, 4096, 4096], P('layer', None, 'row'), may hold values from -0.09375 to 0.09375
- upper_inv: float32 [4, 3, 4096, 4096], P('layer', None, 'row'), may hold values from -0.09375 to 0.09375
- coupling_low: float32 [4, 3, 2048, 4096], P('layer', None, None, 'row'), may hold values from -0.0390625 to 0.0390625
- coupling_up: float32 [4, 3, 4096, 2048], P('layer', None, 'row'), may hold values from -0.1875 to 0.1875
- tile_mask: int32 [4, 3, 16, 32], P('layer', None, None, 'row'), may hold values 0 or 1
- root_inv: float32 [2048, 2048], P('row'), may hold values from -0.125 to 0.125
Outputs:
- sol_sub: float32 [4, 3, 4096, 256], P('layer', None, 'row')
- sol_root: float32 [2048, 256], P('row')
All inputs are finite; a program needn't handle non-finite values. No bound on the sum of `tile_mask` on one device may be relied on, other than what follows from the above.
Results may differ from a plain program's by a relative error of at most 0.0001.
Values sent between devices are 32-bit elements; how exact they have to be, the bound alone decides.
No kernel may reach another device: no remote copies, remote signals or barrier semaphores. Data moves between devices by JAX's collectives and lax.ppermute only.
A program may use at most 128 MiB of HBM per device.

v0:
```python
import jax
import jax.numpy as jnp
from jax import lax
from jax.sharding import PartitionSpec as P

TILE = 128


def masked_tiles(coupling, pattern, tile, flipped):
    blocks, height, breadth = coupling.shape
    shaped = coupling.reshape(blocks, height // tile, tile, breadth // tile, tile)
    if flipped:
        pattern = jnp.transpose(pattern, (0, 2, 1))
    weights = pattern.astype(jnp.float32)[:, :, None, :, None]
    return (shaped * weights).reshape(blocks, height, breadth)


def fold_single(matrix, piece):
    return jnp.dot(
        matrix, piece, precision=lax.Precision.HIGHEST, preferred_element_type=jnp.float32
    )


def body(rhs_sub, rhs_root, lower_inv, upper_inv, coupling_low, coupling_up, tile_mask, root_inv):
    highest = lax.Precision.HIGHEST
    lower = lower_inv[0]
    upper = upper_inv[0]
    vectors = rhs_sub[0]
    blocks = vectors.shape[0]
    results = []
    for index in range(blocks):
        results.append(
            fold_single(lower[index], lax.all_gather(vectors[index], "row", axis=0, tiled=True))
        )
    interim = jnp.stack(results)
    lower_coupling = masked_tiles(coupling_low[0], tile_mask[0], TILE, False)
    local_part = lax.psum_scatter(
        jnp.einsum("kas,ksr->ar", lower_coupling, interim, precision=highest),
        "row",
        scatter_dimension=0,
        tiled=True,
    )
    layer_total = lax.psum(local_part, "layer")
    reduced = rhs_root - layer_total
    columns = root_inv
    sol_root = jnp.dot(
        columns,
        lax.all_gather(reduced, "row", axis=0, tiled=True),
        precision=highest,
        preferred_element_type=jnp.float32,
    )
    upper_coupling = masked_tiles(coupling_up[0], tile_mask[0], TILE, True)
    columns = upper_coupling
    coupled = jnp.einsum(
        "ksa,ar->ksr",
        columns,
        lax.all_gather(sol_root, "row", axis=0, tiled=True),
        precision=highest,
    )
    residue = interim - coupled
    outputs = []
    for index in range(blocks):
        outputs.append(
            fold_single(upper[index], lax.all_gather(residue[index], "row", axis=0, tiled=True))
        )
    solved = jnp.stack(outputs)
    return (solved[None], sol_root)


def solution(mesh):
    return jax.shard_map(
        body,
        mesh=mesh,
        in_specs=(
            P("layer", None, "row", None),
            P("row", None),
            P("layer", None, "row", None),
            P("layer", None, "row", None),
            P("layer", None, None, "row"),
            P("layer", None, "row", None),
            P("layer", None, None, "row"),
            P("row", None),
        ),
        out_specs=(P("layer", None, "row", None), P("row", None)),
        check_vma=False,
    )
```

profile of v0, /device:TPU:1, one launch (start us, length us, event | category | flops | bytes accessed | tf_op | source)
XLA Modules:
  0.0 543.6 jit_solution(12536181070227293686)
XLA Ops:
  7.2 1.8 fusion.65
  9.1 0.0 all-gather.23.cloned.1.call-start
  9.1 0.7 all-gather.23.cloned.1.call-update
  9.9 0.7 all-gather.21.cloned.1.call-update
  10.6 0.7 convert_element_type.19
  11.3 0.1 broadcast_bitcast_fusion
  11.4 48.9 %all-gather.19.cloned.1.call-done = f32[1,1,4096,256]{3,2,1,0:T(8,128)} async-done(((f32[1,1,128,256]{3,2,1,0:T(8,128)}), f32[1,1,4096,256]{3,2,1,0:T(8,128)}) %all-gather.19.cloned.1.call-update) | async-done | bytes 4194320 | tf_op jit(solution)/shard_map/all_gather | solution.py:33
  60.3 4.9 fusion.33
  65.3 42.7 %all-gather.23.cloned.1.call-done = f32[1,1,4096,256]{3,2,1,0:T(8,128)} async-done(((f32[1,1,128,256]{3,2,1,0:T(8,128)}), f32[1,1,4096,256]{3,2,1,0:T(8,128)}) %all-gather.23.cloned.1.call-update) | async-done | bytes 4194320 | tf_op jit(solution)/shard_map/all_gather | solution.py:33
  108.0 4.9 fusion.43
  112.9 42.7 %all-gather.21.cloned.1.call-done = f32[1,1,4096,256]{3,2,1,0:T(8,128)} async-done(((f32[1,1,128,256]{3,2,1,0:T(8,128)}), f32[1,1,4096,256]{3,2,1,0:T(8,128)}) %all-gather.21.cloned.1.call-update) | async-done | bytes 4194320 | tf_op jit(solution)/shard_map/all_gather | solution.py:33
  155.6 5.1 fusion.38
  160.7 5.1 fusion.14
  165.8 76.2 %reduce-scatter.2.cloned.1.call-done = f32[64,256]{1,0:T(8,128)} async-done(((f32[2048,256]{1,0:T(8,128)}), f32[64,256]{1,0:T(8,128)}) %reduce-scatter.2.cloned.1.call-update) | async-done | bytes 65552 | tf_op jit(solution)/shard_map/reduce_scatter | solution.py:37
  242.1 42.6 %all-reduce.2.cloned.1.call-done = f32[64,256]{1,0:T(8,128)} async-done(((f32[64,256]{1,0:T(8,128)}), f32[64,256]{1,0:T(8,128)}) %all-reduce.2.cloned.1.call-update) | async-done | bytes 65552 | tf_op jit(solution)/shard_map/psum | solution.py:43
  284.8 1.5 sub.6
  286.3 0.2 all-gather.17.cloned.1.call-start
  286.5 47.1 %all-gather.15.cloned.1.call-done = f32[2048,256]{1,0:T(8,128)} async-done(((f32[64,256]{1,0:T(8,128)}), f32[2048,256]{1,0:T(8,128)}) %all-gather.15.cloned.1.call-update) | async-done | bytes 2097168 | tf_op jit(solution)/shard_map/all_gather | solution.py:48
  333.6 3.6 convolution_bitcast_fusion
  337.2 0.0 all-gather.25.cloned.1.call-start
  337.2 42.9 %all-gather.17.cloned.1.call-done = f32[2048,256]{1,0:T(8,128)} async-done(((f32[64,256]{1,0:T(8,128)}), f32[2048,256]{1,0:T(8,128)}) %all-gather.17.cloned.1.call-update) | async-done | bytes 2097168 | tf_op jit(solution)/shard_map/all_gather | solution.py:57
  380.1 5.3 fusion.30
  385.4 0.8 fusion.64
  386.2 0.7 all-gather.29.cloned.1.call-update
  386.9 0.5 all-gather.27.cloned.1.call-update
  387.5 44.1 %all-gather.25.cloned.1.call-done = f32[1,4096,256]{2,1,0:T(8,128)} async-done(((f32[1,128,256]{2,1,0:T(8,128)}), f32[1,4096,256]{2,1,0:T(8,128)}) %all-gather.25.cloned.1.call-update) | async-done | bytes 4194320 | tf_op jit(solution)/shard_map/all_gather | solution.py:64
  431.5 9.2 %fusion.48 = f32[1,128,256]{1,2,0:T(8,128)S(1)} fusion(f32[1,3,128,4096]{3,2,1,0:T(8,128)} %param.11, f32[1,4096,256]{2,1,0:T(8,128)} %all-gather.25.cloned.1.call-done), kind=kOutput, calls=%fused_computation.36 | convolution fusion | flops 1610612736 | bytes 6422528 | tf_op jit(solution)/shard_map/dot_general | solution.py:19
  440.7 38.4 %all-gather.29.cloned.1.call-done = f32[1,4096,256]{2,1,0:T(8,128)} async-done(((f32[1,128,256]{2,1,0:T(8,128)}), f32[1,4096,256]{2,1,0:T(8,128)}) %all-gather.29.cloned.1.call-update) | async-done | bytes 4194320 | tf_op jit(solution)/shard_map/all_gather | solution.py:64
  479.2 9.2 %fusion.58 = f32[1,128,256]{1,2,0:T(8,128)S(1)} fusion(f32[1,3,128,4096]{3,2,1,0:T(8,128)} %param.11, f32[1,4096,256]{2,1,0:T(8,128)} %all-gather.29.cloned.1.call-done), kind=kOutput, calls=%fused_computation.38 | convolution fusion | flops 1610612736 | bytes 6422528 | tf_op jit(solution)/shard_map/dot_general | solution.py:19
  488.4 38.3 %all-gather.27.cloned.1.call-done = f32[1,4096,256]{2,1,0:T(8,128)} async-done(((f32[1,128,256]{2,1,0:T(8,128)}), f32[1,4096,256]{2,1,0:T(8,128)}) %all-gather.27.cloned.1.call-update) | async-done | bytes 4194320 | tf_op jit(solution)/shard_map/all_gather | solution.py:64
  526.6 9.2 %fusion.53 = f32[1,128,256]{1,2,0:T(8,128)S(1)} fusion(f32[1,3,128,4096]{3,2,1,0:T(8,128)} %param.11, f32[1,4096,256]{2,1,0:T(8,128)} %all-gather.27.cloned.1.call-done), kind=kOutput, calls=%fused_computation.37 | convolution fusion | flops 1610612736 | bytes 6422528 | tf_op jit(solution)/shard_map/dot_general | solution.py:19
  535.9 0.9 copy.10
  (22 shorter events, 0.4 us)
Async XLA Ops:
  7.2 326.4 %copy-start = (f32[64,2048]{1,0:T(8,128)S(1)}, f32[64,2048]{1,0:T(8,128)}, u32[]{:S(2)}) copy-start(f32[64,2048]{1,0:T(8,128)} %param.15) | copy-start | bytes 1572868
  7.2 53.2 %all-gather.19.cloned.1.call-start = ((), (), s32[]{:S(2)}) async-start(), calls=%async_computation.5 | async-start | bytes 4325376 | tf_op jit(solution)/shard_map/all_gather | solution.py:33
  9.1 98.9 %all-gather.23.cloned.1.call-start = ((), (), s32[]{:S(2)}) async-start(), calls=%async_computation.7 | async-start | bytes 4325376 | tf_op jit(solution)/shard_map/all_gather | solution.py:33
  9.8 145.7 %all-gather.21.cloned.1.call-start = ((), (), s32[]{:S(2)}) async-start(), calls=%async_computation.6 | async-start | bytes 4325376 | tf_op jit(solution)/shard_map/all_gather | solution.py:33
  10.6 231.5 %reduce-scatter.2.cloned.1.call-start = ((), (), s32[]{:S(2)}) async-start(), calls=%async_computation.1 | async-start | bytes 2162688 | tf_op jit(solution)/shard_map/reduce_scatter | solution.py:37
  155.6 5.1 copy-start.1
  160.6 124.1 %copy-start.2 = (f32[64,256]{1,0:T(8,128)S(1)}, f32[64,256]{1,0:T(8,128)}, u32[]{:S(2)}) copy-start(f32[64,256]{1,0:T(8,128)} %param.9) | copy-start | bytes 196612
  165.8 119.0 %all-reduce.2.cloned.1.call-start = ((), (), s32[]{:S(2)}) async-start(), calls=%async_computation.2 | async-start | bytes 131072 | tf_op jit(solution)/shard_map/psum | solution.py:43
  242.1 91.5 %all-gather.15.cloned.1.call-start = ((), (), s32[]{:S(2)}) async-start(), calls=%async_computation.3 | async-start | bytes 2162688 | tf_op jit(solution)/shard_map/all_gather | solution.py:48
  286.3 93.8 %all-gather.17.cloned.1.call-start = ((), (), s32[]{:S(2)}) async-start(), calls=%async_computation.4 | async-start | bytes 2162688 | tf_op jit(solution)/shard_map/all_gather | solution.py:57
  337.2 94.4 %all-gather.25.cloned.1.call-start = ((), (), s32[]{:S(2)}) async-start(), calls=%async_computation.8 | async-start | bytes 4325376 | tf_op jit(solution)/shard_map/all_gather | solution.py:64
  386.1 93.0 %all-gather.29.cloned.1.call-start = ((), (), s32[]{:S(2)}) async-start(), calls=%async_computation.10 | async-start | bytes 4325376 | tf_op jit(solution)/shard_map/all_gather | solution.py:64
  386.9 139.8 %all-gather.27.cloned.1.call-start = ((), (), s32[]{:S(2)}) async-start(), calls=%async_computation.9 | async-start | bytes 4325376 | tf_op jit(solution)/shard_map/all_gather | solution.py:64
Sparse Core Ops, SparseCore 0:
  10.8 49.4 all-gather.18
  62.6 45.3 all-gather.22
  110.2 45.3 all-gather.20
  165.9 76.1 reduce-scatter.1
  244.2 40.5 all-reduce.1
  287.5 46.0 all-gather.14
  337.3 42.7 all-gather.16
  386.3 45.2 all-gather.24
  433.8 45.3 all-gather.28
  481.3 45.3 all-gather.26
where the time goes:
time: 544 us
  waiting for transfers between devices  467 us (86%)
  matrix products  56.3 us (10%)
  between operations  14.3 us (3%)
    all_gather x3, waiting for transfers between devices, body(): lax.all_gather(vectors[index], 'row', axis=0, tiled=True)  134 us
    all_gather x3, waiting for transfers between devices, body(): lax.all_gather(residue[index], 'row', axis=0, tiled=True)  121 us
    reduce_scatter x1, waiting for transfers between devices, body(): lax.psum_scatter(jnp.einsum('kas,ksr->ar', lower_coupling, interim, preci...  76.2 us
    all_gather x1, waiting for transfers between devices, body(): lax.all_gather(reduced, 'row', axis=0, tiled=True)  47.1 us
    all_gather x1, waiting for transfers between devices, body(): lax.all_gather(sol_root, 'row', axis=0, tiled=True)  42.9 us
    psum x1, waiting for transfers between devices, body(): layer_total = lax.psum(local_part, 'layer')  42.6 us
    dot_general x6, matrix products, fold_single(): jnp.dot(matrix, piece, precision=lax.Precision.HIGHEST, preferred_element...  42.4 us
  transfers between devices with their start and end apart: 10, of which 10 were waited for; matrix products, arithmetic and copies ran while one was open for 5% of the time, Pallas kernels for 0%

commit v1 on v0

--- a/solution.py
+++ b/solution.py
@@ -4,6 +4,11 @@
 from jax.sharding import PartitionSpec as P
 
 TILE = 128
+
+
+def gather_over(x, axis, dim):
+    sent = jnp.stack([x] * lax.axis_size(axis))
+    return jnp.concatenate(lax.all_to_all(sent, axis, 0, 0), axis=dim)
 
 
 def masked_tiles(coupling, pattern, tile, flipped):
@@ -60,9 +65,7 @@
     residue = interim - coupled
     outputs = []
     for index in range(blocks):
-        outputs.append(
-            fold_single(upper[index], lax.all_gather(residue[index], "row", axis=0, tiled=True))
-        )
+        outputs.append(fold_single(upper[index], gather_over(residue[index], "row", 0)))
     solved = jnp.stack(outputs)
     return (solved[None], sol_root)
 

time: 544 us -> 575 us (1.057)
  blocking collectives: 0 us -> 111 us
  waiting for transfers between devices: 467 us -> 378 us
    all_gather x3 -> x0, waiting for transfers between devices: 121 us -> none  [body(): lax.all_gather(residue[index], 'row', axis=0, tiled=True)]
    all_to_all x0 -> x2, blocking collectives: none -> 111 us  [gather_over(): return jnp.concatenate(lax.all_to_all(sent, axis, 0, 0), axis=dim)]
    all_to_all x0 -> x1, waiting for transfers between devices: none -> 32.9 us  [gather_over(): return jnp.concatenate(lax.all_to_all(sent, axis, 0, 0), axis=dim)]
  transfers between devices with their start and end apart: 10 -> 8, of which waited for: 10 -> 8; matrix products, arithmetic and copies ran while one was open for 5% -> 5% of each run, Pallas kernels for 0% -> 0%
where the time goes in v1:
time: 575 us; the launch traced here: 572 us
  waiting for transfers between devices  378 us (66%)
  blocking collectives  111 us (19%)
  matrix products  55.7 us (10%)
  between operations  14.3 us (2%)
  local copies, waits for them, and re-layouts  6.26 us (1%)
    all_gather x3, waiting for transfers between devices, body(): lax.all_gather(vectors[index], 'row', axis=0, tiled=True)  134 us
    all_to_all x2, blocking collectives, gather_over(): return jnp.concatenate(lax.all_to_all(sent, axis, 0, 0), axis=dim)  111 us
    reduce_scatter x1, waiting for transfers between devices, body(): lax.psum_scatter(jnp.einsum('kas,ksr->ar', lower_coupling, interim, preci...  76.2 us
    all_gather x1, waiting for transfers between devices, body(): lax.all_gather(reduced, 'row', axis=0, tiled=True)  47.1 us
    all_gather x1, waiting for transfers between devices, body(): lax.all_gather(sol_root, 'row', axis=0, tiled=True)  42.9 us
    psum x1, waiting for transfers between devices, body(): layer_total = lax.psum(local_part, 'layer')  42.6 us
    dot_general x6, matrix products, fold_single(): jnp.dot(matrix, piece, precision=lax.Precision.HIGHEST, preferred_element...  41.8 us
    all_to_all x1, waiting for transfers between devices, gather_over(): return jnp.concatenate(lax.all_to_all(sent, axis, 0, 0), axis=dim)  32.9 us
  transfers between devices with their start and end apart: 8, of which 8 were waited for; matrix products, arithmetic and copies ran while one was open for 5% of the time, Pallas kernels for 0%

profile of v1, /device:TPU:1, one launch (start us, length us, event | category | flops | bytes accessed | tf_op | source)
XLA Modules:
  0.0 571.8 jit_solution(9698089775046689618)
XLA Ops:
  7.2 1.8 fusion.55
  9.1 0.7 all-gather.17.cloned.1.call-update
  9.9 0.7 all-gather.15.cloned.1.call-update
  10.6 0.7 convert_element_type.19
  11.3 0.1 broadcast_bitcast_fusion
  11.4 48.9 %all-gather.13.cloned.1.call-done = f32[1,1,4096,256]{3,2,1,0:T(8,128)} async-done(((f32[1,1,128,256]{3,2,1,0:T(8,128)}), f32[1,1,4096,256]{3,2,1,0:T(8,128)}) %all-gather.13.cloned.1.call-update) | async-done | bytes 4194320 | tf_op jit(solution)/shard_map/all_gather | solution.py:38
  60.3 4.9 fusion.39
  65.3 42.7 %all-gather.17.cloned.1.call-done = f32[1,1,4096,256]{3,2,1,0:T(8,128)} async-done(((f32[1,1,128,256]{3,2,1,0:T(8,128)}), f32[1,1,4096,256]{3,2,1,0:T(8,128)}) %all-gather.17.cloned.1.call-update) | async-done | bytes 4194320 | tf_op jit(solution)/shard_map/all_gather | solution.py:38
  108.0 4.9 fusion.49
  112.9 42.7 %all-gather.15.cloned.1.call-done = f32[1,1,4096,256]{3,2,1,0:T(8,128)} async-done(((f32[1,1,128,256]{3,2,1,0:T(8,128)}), f32[1,1,4096,256]{3,2,1,0:T(8,128)}) %all-gather.15.cloned.1.call-update) | async-done | bytes 4194320 | tf_op jit(solution)/shard_map/all_gather | solution.py:38
  155.6 5.1 fusion.44
  160.7 5.1 fusion.8
  165.8 0.0 all-reduce.2.cloned.1.call-start
  165.8 76.2 %reduce-scatter.2.cloned.1.call-done = f32[64,256]{1,0:T(8,128)} async-done(((f32[2048,256]{1,0:T(8,128)}), f32[64,256]{1,0:T(8,128)}) %reduce-scatter.2.cloned.1.call-update) | async-done | bytes 65552 | tf_op jit(solution)/shard_map/reduce_scatter | solution.py:42
  242.1 42.6 %all-reduce.2.cloned.1.call-done = f32[64,256]{1,0:T(8,128)} async-done(((f32[64,256]{1,0:T(8,128)}), f32[64,256]{1,0:T(8,128)}) %all-reduce.2.cloned.1.call-update) | async-done | bytes 65552 | tf_op jit(solution)/shard_map/psum | solution.py:48
  284.8 1.5 sub.6
  286.3 0.2 all-gather.11.cloned.1.call-start
  286.5 47.1 %all-gather.9.cloned.1.call-done = f32[2048,256]{1,0:T(8,128)} async-done(((f32[64,256]{1,0:T(8,128)}), f32[2048,256]{1,0:T(8,128)}) %all-gather.9.cloned.1.call-update) | async-done | bytes 2097168 | tf_op jit(solution)/shard_map/all_gather | solution.py:53
  333.6 3.6 convolution_bitcast_fusion
  337.1 42.9 %all-gather.11.cloned.1.call-done = f32[2048,256]{1,0:T(8,128)} async-done(((f32[64,256]{1,0:T(8,128)}), f32[2048,256]{1,0:T(8,128)}) %all-gather.11.cloned.1.call-update) | async-done | bytes 2097168 | tf_op jit(solution)/shard_map/all_gather | solution.py:62
  380.1 5.3 fusion.27
  385.4 0.5 stack.37
  385.9 55.9 %all_to_all.15 = f32[32,128,256]{2,1,0:T(8,128)} all-to-all(f32[32,128,256]{2,1,0:T(8,128)S(1)} %stack.37), channel_id=1, replica_groups=mesh['layer'=4,'row'=32] {'row'}, dimensions={0} | all-to-all | bytes 8388608 | tf_op jit(solution)/shard_map/all_to_all | solution.py:11
  441.8 0.5 stack.41
  442.2 54.6 %all_to_all.16 = f32[32,128,256]{2,1,0:T(8,128)} all-to-all(f32[32,128,256]{2,1,0:T(8,128)S(1)} %stack.41), channel_id=1, replica_groups=mesh['layer'=4,'row'=32] {'row'}, dimensions={0} | all-to-all | bytes 8388608 | tf_op jit(solution)/shard_map/all_to_all | solution.py:11
  496.9 2.5 stack.39
  499.3 4.9 all-to-all-start.1
  504.2 9.3 %fusion.30 = f32[1,128,256]{1,2,0:T(8,128)S(1)} fusion(f32[4096,256]{1,0:T(8,128)} %bitcast.106, f32[1,3,128,4096]{3,2,1,0:T(8,128)} %param.11), kind=kOutput, calls=%fused_computation.30 | convolution fusion | flops 1610612736 | bytes 6422528 | tf_op jit(solution)/shard_map/dot_general | solution.py:24
  513.6 8.4 %fusion.36 = f32[1,128,256]{1,2,0:T(8,128)S(1)} fusion(f32[4096,256]{1,0:T(8,128)S(1)} %bitcast.107, f32[1,3,128,4096]{3,2,1,0:T(8,128)} %param.11), kind=kOutput, calls=%fused_computation.32 | convolution fusion | flops 1610612736 | bytes 6422528 | tf_op jit(solution)/shard_map/dot_general | solution.py:24
  521.9 32.9 %all-to-all-done.1 = f32[32,128,256]{2,1,0:T(8,128)} async-done(((f32[32,128,256]{2,1,0:T(8,128)}), f32[32,128,256]{2,1,0:T(8,128)}, u32[]{:S(2)}, u32[]{:S(2)}) %all-to-all-start.1) | async-done | bytes 4194336 | tf_op jit(solution)/shard_map/all_to_all | solution.py:11
  554.8 9.2 %fusion.33 = f32[1,128,256]{1,2,0:T(8,128)S(1)} fusion(f32[4096,256]{1,0:T(8,128)} %bitcast.20, f32[1,3,128,4096]{3,2,1,0:T(8,128)} %param.11), kind=kOutput, calls=%fused_computation.31 | convolution fusion | flops 1610612736 | bytes 6422528 | tf_op jit(solution)/shard_map/dot_general | solution.py:24
  564.1 0.9 copy.10
  (22 shorter events, 0.4 us)
Async XLA Ops:
  7.2 326.4 %copy-start = (f32[64,2048]{1,0:T(8,128)S(1)}, f32[64,2048]{1,0:T(8,128)}, u32[]{:S(2)}) copy-start(f32[64,2048]{1,0:T(8,128)} %param.15) | copy-start | bytes 1572868
  7.2 53.2 %all-gather.13.cloned.1.call-start = ((), (), s32[]{:S(2)}) async-start(), calls=%async_computation.8 | async-start | bytes 4325376 | tf_op jit(solution)/shard_map/all_gather | solution.py:38
  9.1 98.9 %all-gather.17.cloned.1.call-start = ((), (), s32[]{:S(2)}) async-start(), calls=%async_computation.10 | async-start | bytes 4325376 | tf_op jit(solution)/shard_map/all_gather | solution.py:38
  9.8 145.7 %all-gather.15.cloned.1.call-start = ((), (), s32[]{:S(2)}) async-start(), calls=%async_computation.9 | async-start | bytes 4325376 | tf_op jit(solution)/shard_map/all_gather | solution.py:38
  10.6 231.5 %reduce-scatter.2.cloned.1.call-start = ((), (), s32[]{:S(2)}) async-start(), calls=%async_computation.4 | async-start | bytes 2162688 | tf_op jit(solution)/shard_map/reduce_scatter | solution.py:42
  155.6 5.1 copy-start.2
  160.6 124.1 %copy-start.3 = (f32[64,256]{1,0:T(8,128)S(1)}, f32[64,256]{1,0:T(8,128)}, u32[]{:S(2)}) copy-start(f32[64,256]{1,0:T(8,128)} %param.9) | copy-start | bytes 196612
  165.8 119.0 %all-reduce.2.cloned.1.call-start = ((), (), s32[]{:S(2)}) async-start(), calls=%async_computation.5 | async-start | bytes 131072 | tf_op jit(solution)/shard_map/psum | solution.py:48
  242.1 91.5 %all-gather.9.cloned.1.call-start = ((), (), s32[]{:S(2)}) async-start(), calls=%async_computation.6 | async-start | bytes 2162688 | tf_op jit(solution)/shard_map/all_gather | solution.py:53
  286.3 93.8 %all-gather.11.cloned.1.call-start = ((), (), s32[]{:S(2)}) async-start(), calls=%async_computation.7 | async-start | bytes 2162688 | tf_op jit(solution)/shard_map/all_gather | solution.py:62
  499.3 55.5 %all-to-all-start.1 = ((f32[32,128,256]{2,1,0:T(8,128)}), f32[32,128,256]{2,1,0:T(8,128)}, u32[]{:S(2)}, u32[]{:S(2)}) async-start(f32[32,128,256]{2,1,0:T(8,128)} %stack.39), calls=%async_computation.2 | async-start | bytes 8388608 | tf_op jit(solution)/shard_map/all_to_all | solution.py:11
  504.2 9.4 %copy-start.1 = (f32[32,128,256]{2,1,0:T(8,128)S(1)}, f32[32,128,256]{2,1,0:T(8,128)}, u32[]{:S(2)}) copy-start(f32[32,128,256]{2,1,0:T(8,128)} %all_to_all.16) | copy-start | bytes 12582916
Sparse Core Ops, SparseCore 0:
  10.8 49.4 all-gather.12
  62.6 45.3 all-gather.16
  110.2 45.3 all-gather.14
  165.9 76.1 reduce-scatter.1
  244.2 40.5 all-reduce.1
  287.5 46.0 all-gather.8
  337.3 42.7 all-gather.10
